TPU v7x, 32 devices: a whole 2x2x4 slice. The times are simulated.
32 devices in a mesh: grp: 2 (over y), row: 4 (over z), col: 2 (over x), pole: 2 (over core).
Axes of the slice: x: 2, y: 2, z: 4, core: 2. Of those that a mesh axis runs over, the one named last changes fastest.
Arguments:
- inverse_front: bfloat16 [4, 2, 8192, 4096], P(('grp', 'pole'), None, 'row', 'col'), parts along dimension 0, may hold values from -6 to 6
- tile_mask: int32 [128, 32], P(('grp', 'row'), 'col'), parts along dimension 0, may hold values 0 or 1
- lower_panel: bfloat16 [2, 4, 2, 256, 4096], P(None, ('grp', 'pole'), None, 'row', 'col'), parts along dimension 1, may hold values from -0.09375 to 0.09375
- upper_panel: bfloat16 [2, 4, 2, 256, 8192], P(None, ('grp', 'pole'), None, 'col', 'row'), parts along dimension 1, may hold values from -0.0625 to 0.0625
- pivots: float32 [2, 4, 256], P(None, ('grp', 'pole')), parts along dimension 1, may hold values from 0.01 to 0.1
- pole_weight: float32 [2, 128], P(None, 'grp'), parts along dimension 1, may hold values from -4 to 4
- pole_slot: int32 [4], P('grp'), parts along dimension 0, may hold values from 0 to 63
- supernode: int32 [1024], P('grp'), parts along dimension 0, may hold values from 0 to 127, never falling along the last dimension, each value on 1 to 64 neighbouring positions
Outputs:
- updated_front: bfloat16 [4, 2, 8192, 4096], P(('grp', 'pole'), None, 'row', 'col'), parts along dimension 0
- density: float32 [4, 256, 256], P('grp', None, 'col'), parts along dimension 0
There are 2 independent parts, one for each index of `grp`. A program takes and returns all parts, laid end to end along the dimension named above; each array names one. Nothing has to cross between parts.
Inputs may be any that keep to these rules, and one draw needn't show every extreme that they name: `tile_mask`: 1 marks a present tile of 128 x 128 entries. `pole_slot`: each slot names one pole of the table. Never falling along the 512 columns; each supernode spans at most 64 columns.
All inputs are finite; a program needn't handle non-finite values. No bound on the sum of `tile_mask` on one device may be relied on, other than what follows from the above.
Results may differ from a plain program's by a relative error of at most 0.035.
Values may be sent and summed in bfloat16 or wider, within the bound.
No kernel may reach another device: no remote copies, remote signals or barrier semaphores. Data moves between devices by JAX's collectives and lax.ppermute only.
A program may use at most 192 MiB of HBM per device.

v0:
```python
import functools

import jax
import jax.numpy as jnp
from jax import lax
from jax.experimental import pallas as pl
from jax.experimental.pallas import tpu as pltpu
from jax.sharding import PartitionSpec as P


F32 = jnp.float32
BF16 = jnp.bfloat16
CONTRACT_LAST = (((1,), (1,)), ((), ()))
VMEM_LIMIT = 48 << 20


def whole(shape):
    return pl.BlockSpec(
        shape, lambda *_: (0,) * len(shape), pipeline_mode=pl.Buffered(1)
    )


def call(kernel, grid, scalars, operands, outs, scratch, flops, aliases=None):
    moved = sum(a.size * a.dtype.itemsize for a, _ in operands)
    moved += sum(o.size * o.dtype.itemsize for o, _ in outs)
    shapes = [o for o, _ in outs]
    specs = [s for _, s in outs]
    return pl.pallas_call(
        kernel,
        grid_spec=pltpu.PrefetchScalarGridSpec(
            num_scalar_prefetch=len(scalars),
            grid=grid,
            in_specs=[s for _, s in operands],
            out_specs=specs,
            scratch_shapes=scratch,
        ),
        out_shape=shapes,
        input_output_aliases=aliases or {},
        compiler_params=pltpu.CompilerParams(vmem_limit_bytes=VMEM_LIMIT),
        cost_estimate=pl.CostEstimate(
            flops=flops, bytes_accessed=moved, transcendentals=0
        ),
    )(*scalars, *[a for a, _ in operands])


ANY = pl.BlockSpec(memory_space=pl.ANY)


def assemble(owners, inner, pieces, sizes, full):
    share = pieces[0].shape[1]
    width = share * len(sizes)
    at = 0
    for k, size in enumerate(sizes):
        start = pl.multiple_of(owners[k] * share, share)
        for part in range(2):
            piece = pieces[at][part]
            if size == 2:
                piece = jnp.where(inner[0] != 0, piece, pieces[at + 1][part])
            full[pl.ds(part * width + start, share), :] = piece
        at += size


def flat(slots):
    return [piece for slot in slots for piece in slot]


def sizes_of(slots):
    return tuple(len(slot) for slot in slots)


def first_step(function):
    pl.when(pl.program_id(0) == 0)(function)


def masked_tiles(mask, source, target, tile, row_tile, col_tile):
    rows, cols = source.shape[1:]
    for part in range(2):
        for i in range(rows // tile):
            for k in range(cols // tile):
                keep = mask[row_tile + i, col_tile + k] != 0
                at = (
                    part,
                    slice(i * tile, (i + 1) * tile),
                    slice(k * tile, (k + 1) * tile),
                )
                block = source[at]
                target[at] = jnp.where(keep, block, jnp.zeros_like(block))


def negative_product(upper, masked):
    width = upper.shape[0] // 2
    by_real = jnp.dot(upper, masked[0], preferred_element_type=F32)
    by_imag = jnp.dot(upper, masked[1], preferred_element_type=F32)
    return (
        (by_imag[width:] - by_real[:width]).astype(BF16),
        (-(by_imag[:width] + by_real[width:])).astype(BF16),
    )


def y_kernel(mask, order, front, *rest, tile, count):
    slots, (*outs, masked) = rest[:count], rest[count:]
    step = pl.program_id(0)
    per_piece = pl.num_programs(0) // PIECES
    block = order[step // per_piece] * per_piece + step % per_piece
    masked_tiles(mask, front, masked, tile, 0, block * (front.shape[2] // tile))
    for s, slot in enumerate(slots):
        upper = slot[...].reshape(2 * slot.shape[1], slot.shape[2])
        y = negative_product(upper, masked)
        for k in range(2):

            @pl.when(step // (2 * per_piece) == k)
            def _(y_ref=outs[2 * s + k], y=y):
                y_ref[0, 0], y_ref[0, 1] = y


def y_parts(front, mask, order, slots, tile):
    _, rows, cols = front.shape
    share = slots[0].shape[1]
    span = cols // PIECES
    block = min(256, span)
    per_piece = span // block

    def out_spec(k):
        def place(j, *_):
            at = jnp.clip(j - 2 * k * per_piece, 0, 2 * per_piece - 1)
            return (at // per_piece, 0, 0, at % per_piece)

        return pl.BlockSpec((1, 2, share, block), place)

    def column(j, mask, order):
        return (0, 0, order[j // per_piece] * per_piece + j % per_piece)

    outs = [(jax.ShapeDtypeStruct((2, 2, share, span), BF16), out_spec(k)) for k in range(2)]
    return call(
        functools.partial(y_kernel, tile=tile, count=len(slots)),
        (cols // block,),
        (mask, order),
        [(front, pl.BlockSpec((2, rows, block), column))] + [(s, whole(s.shape)) for s in slots],
        outs * len(slots),
        [pltpu.VMEM((2, rows, block), BF16)],
        8 * share * len(slots) * rows * cols,
    )


def x_kernel(mask, owners, inner, front, *rest, tile, first, sizes):
    *pieces, x_ref, masked, lower = rest

    @first_step
    def _():
        assemble(owners, inner, pieces, sizes, lower)

    step = first + pl.program_id(0)
    masked_tiles(mask, front, masked, tile, step * (front.shape[1] // tile), 0)
    width = lower.shape[0] // 2
    by_real = lax.dot_general(
        masked[0], lower[...], CONTRACT_LAST, preferred_element_type=F32
    )
    by_imag = lax.dot_general(
        masked[1], lower[...], CONTRACT_LAST, preferred_element_type=F32
    )
    x_ref[0] = (by_imag[:, width:] - by_real[:, :width]).astype(BF16)
    x_ref[1] = (-(by_imag[:, :width] + by_real[:, width:])).astype(BF16)


def x_part(front, mask, owners, inner, slots, start, span, tile):
    _, _, cols = front.shape
    width = slots[0][0].shape[1] * len(slots)
    block = min(256, span)
    first = start // block
    return call(
        functools.partial(x_kernel, tile=tile, first=first, sizes=sizes_of(slots)),
        (span // block,),
        (mask, owners, inner),
        [(front, pl.BlockSpec((2, block, cols), lambda j, *_: (0, first + j, 0)))]
        + [(s, whole(s.shape)) for s in flat(slots)],
        [
            (
                jax.ShapeDtypeStruct((2, span, width), BF16),
                pl.BlockSpec((2, block, width), lambda j, *_: (0, j, 0)),
            )
        ],
        [
            pltpu.VMEM((2, block, cols), BF16),
            pltpu.VMEM((2 * width, cols), BF16),
        ],
        8 * width * span * cols,
    )[0]


def scale(own, other, pivot):
    x = add(own, other)
    return (x.astype(F32) * pivot[None]).astype(BF16)


def density_kernel(owners, inner, weight, *rest, count, sizes):
    *pieces, out, upper = rest
    parts, pieces = pieces[:count], pieces[count:]
    assemble(owners, inner, pieces, sizes, upper)
    width = upper.shape[0] // 2
    shape = (2 * width, width)
    by_real, by_imag = jnp.zeros(shape, F32), jnp.zeros(shape, F32)
    start = 0
    for x in parts:
        piece = upper[:, start : start + x.shape[1]]
        start += x.shape[1]
        by_real += jnp.dot(piece, x[0], preferred_element_type=F32)
        by_imag += jnp.dot(piece, x[1], preferred_element_type=F32)
    real = by_real[:width] - by_imag[width:]
    imag = by_imag[:width] + by_real[width:]
    out[...] = (weight[1] * imag - weight[0] * real).astype(BF16)


def density_part(parts, owners, inner, slots, weight):
    width = parts[0].shape[2]
    rows = slots[0][0].shape[2]
    shape = (width, width)
    return call(
        functools.partial(density_kernel, count=len(parts), sizes=sizes_of(slots)),
        (1,),
        (owners, inner, weight),
        [(a, whole(a.shape)) for a in (*parts, *flat(slots))],
        [(jax.ShapeDtypeStruct(shape, BF16), whole(shape))],
        [pltpu.VMEM((2 * width, rows), BF16)],
        8 * width * width * rows,
    )[0]


def fill_right(right, start, real, imag):
    width, cols = right.shape[0] // 2, right.shape[1] // 2
    share = real.shape[0]
    right[pl.ds(start, share), :cols] = real
    right[pl.ds(start, share), cols:] = imag
    right[pl.ds(width + start, share), :cols] = -imag
    right[pl.ds(width + start, share), cols:] = real


def update_rows(mask, scaled, right, front, new, masked, tile, row_tile, col_tile):
    _, cols = front.shape[1:]
    span = min(256, *[left.shape[1] for left in scaled])
    blocks = [(left, at) for left in scaled for at in range(0, left.shape[1], span)]
    for i, (left, start) in enumerate(blocks):
        at_left = slice(start, start + span)
        both = jnp.concatenate([left[0, at_left, :], left[1, at_left, :]], axis=1)
        product = jnp.dot(both, right[...], preferred_element_type=F32)
        for a in range(span // tile):
            for k in range(cols // tile):
                keep = mask[row_tile + i * (span // tile) + a, col_tile + k]
                factor = keep.astype(F32)
                for part in range(2):
                    at = (
                        part,
                        slice(i * span + a * tile, i * span + (a + 1) * tile),
                        slice(k * tile, (k + 1) * tile),
                    )
                    term = product[
                        a * tile : (a + 1) * tile,
                        part * cols + k * tile : part * cols + (k + 1) * tile,
                    ]
                    value = (front[at].astype(F32) + factor * term).astype(BF16)
                    new[at] = value
                    if masked is not None:
                        masked[at] = jnp.where(keep != 0, value, jnp.zeros_like(value))


def update_y_kernel(mask, owners, inner, order, front, y, *rest, tile, piece, parts, alias, sizes):
    scaled, rest = rest[:parts], rest[parts + alias :]
    *gathered, new, y_ref, masked, right, upper = rest

    @first_step
    def _():
        assemble(owners, inner, gathered, sizes, upper)

    for k in range(y.shape[0]):
        share = y.shape[2]
        fill_right(right, pl.multiple_of(owners[k] * share, share), y[k, 0], y[k, 1])
    block = order[piece] * pl.num_programs(0) + pl.program_id(0)
    update_rows(
        mask, scaled, right, front, new, masked, tile, 0, block * (front.shape[2] // tile)
    )
    y_ref[0], y_ref[1] = negative_product(upper[...], masked)


def update_y(front, target, mask, owners, inner, order, scaled, y, slots, piece, tile):
    _, rows, cols = front.shape
    share = slots[0][0].shape[1]
    width = share * len(slots)
    span = cols // PIECES
    block = min(256, span)
    per_piece = span // block

    def column(j, mask, owners, inner, order):
        return (0, 0, order[piece] * per_piece + j)

    at_piece = pl.BlockSpec((2, rows, block), column)
    term = pl.BlockSpec((*y.shape[:3], block), lambda j, *_: (0, 0, 0, j))
    operands = [(front, at_piece), (y, term)]
    operands += [(s, whole(s.shape)) for s in scaled]
    aliases = {}
    if target is not None:
        aliases = {4 + len(operands): 0}
        operands.append((target, ANY))
    operands += [(s, whole(s.shape)) for s in flat(slots)]
    return call(
        functools.partial(
            update_y_kernel,
            tile=tile,
            piece=piece,
            parts=len(scaled),
            alias=int(target is not None),
            sizes=sizes_of(slots),
        ),
        (per_piece,),
        (mask, owners, inner, order),
        operands,
        [
            (jax.ShapeDtypeStruct(front.shape, BF16), at_piece),
            (
                jax.ShapeDtypeStruct((2, width, span), BF16),
                pl.BlockSpec((2, width, block), lambda j, *_: (0, 0, j)),
            ),
        ],
        [
            pltpu.VMEM((2, rows, block), BF16),
            pltpu.VMEM((2 * width, 2 * block), BF16),
            pltpu.VMEM((2 * width, rows), BF16),
        ],
        16 * width * rows * span,
        aliases,
    )


def update_kernel(mask, order, front, y, *rest, tile, piece):
    *scaled, new, right = rest
    fill_right(right, 0, y[0], y[1])
    block = order[piece] * pl.num_programs(0) + pl.program_id(0)
    col_tile = block * (front.shape[2] // tile)
    update_rows(mask, scaled, right, front, new, None, tile, 0, col_tile)


def update(front, mask, order, scaled, y, piece, tile):
    _, rows, cols = front.shape
    width = scaled[0].shape[2]
    span = cols // PIECES
    block = min(256, span)
    per_piece = span // block

    def column(j, mask, order):
        return (0, 0, order[piece] * per_piece + j)

    at_piece = pl.BlockSpec((2, rows, block), column)
    return call(
        functools.partial(update_kernel, tile=tile, piece=piece),
        (per_piece,),
        (mask, order),
        [(front, at_piece), (y, pl.BlockSpec((2, width, block), lambda j, *_: (0, 0, j)))]
        + [(s, whole(s.shape)) for s in scaled],
        [(jax.ShapeDtypeStruct(front.shape, BF16), at_piece)],
        [pltpu.VMEM((2 * width, 2 * block), BF16)],
        8 * width * rows * span,
        {2: 0},
    )[0]


def shift(value, axis, by):
    n = lax.axis_size(axis)
    return lax.ppermute(value, axis, [(i, (i + by) % n) for i in range(n)])


def gather(piece, axis):
    n = lax.axis_size(axis)
    slots = [None] * n
    slots[0] = (piece,)
    ahead = behind = piece
    for k in range(1, n // 2 + 1):
        ahead = shift(ahead, axis, 1)
        slots[k] = (ahead,)
        if n - k > k:
            behind = shift(behind, axis, -1)
            slots[n - k] = (behind,)
    owners = (lax.axis_index(axis) - jnp.arange(n, dtype=jnp.int32)) % n
    return owners.astype(jnp.int32), slots


def gather_line(piece, axis):
    n = lax.axis_size(axis)
    if n != 4:
        return gather(piece, axis)
    swap, across, outward = [(0, 1), (1, 0), (2, 3), (3, 2)], [(1, 2), (2, 1)], [(1, 0), (2, 3)]
    near = lax.ppermute(piece, axis, swap)
    mid0 = lax.ppermute(piece, axis, across)
    mid1 = lax.ppermute(near, axis, across)
    out0 = lax.ppermute(mid0, axis, outward)
    out1 = lax.ppermute(mid1, axis, outward)
    me = lax.axis_index(axis)
    first = jnp.where(me < 2, 2, 1)
    owners = jnp.stack([me, me ^ 1, first, first ^ 1]).astype(jnp.int32)
    return owners, [(piece,), (near,), (mid0, out0), (mid1, out1)]


def add(left, right):
    return (left.astype(F32) + right.astype(F32)).astype(BF16)


def flip(value, bit):
    pairs = [(i, i ^ bit) for i in range(lax.axis_size("row"))]
    return lax.ppermute(value, "row", pairs)


def add3(one, two, three):
    return (one.astype(F32) + two.astype(F32) + three.astype(F32)).astype(BF16)


def stacked(function, *lists):
    return jnp.stack([function(*terms) for terms in zip(*lists)])


def spread(own):
    near = flip(own, 1)
    far = flip(own, 2)
    return [near, flip(far, 1), far, own]


def sum_first(terms):
    sent, kept = terms[0::2], terms[1::2]
    if lax.axis_size("row") != 4:
        sums = [lax.psum(jnp.concatenate(pair), "row") for pair in zip(sent, kept)]
        return [jnp.stack([total[k] for total in sums]) for k in range(PIECES)]
    got = [flip(y, 1) for y in sent]
    passed = stacked(add, [k[0] for k in kept], [g[1] for g in got])
    other = flip(passed, 2)
    own = stacked(add3, [k[1] for k in kept], [g[0] for g in got], list(other))
    return spread(own)


def sum_next(terms):
    if lax.axis_size("row") != 4:
        return [lax.psum(y, "row") for y in terms]
    got = [flip(y, 1) for y in terms[:2]]
    passed = add(terms[2], got[1])
    other = flip(passed, 2)
    own = add3(terms[3], got[0], other)
    return spread(own)


def terms_over_col(part):
    if lax.axis_size("col") == 2:
        return part, shift(part, "col", 1)
    total = lax.psum(part, "col")
    return total, jnp.zeros_like(total)


def exchange_sum(value, axis):
    n = lax.axis_size(axis)
    if n & (n - 1):
        return lax.psum(value, axis)
    step = 1
    while step < n:
        partner = [(i, i ^ step) for i in range(n)]
        other = lax.ppermute(value, axis, partner)
        value = add(value, other)
        step *= 2
    return value


def reduce_density(part):
    n = lax.axis_size("col")
    share = part.shape[2] // n
    narrow = part
    me = lax.axis_index("col")
    if n == 2:
        mine = lax.dynamic_slice_in_dim(narrow, me * share, share, 2)
        theirs = lax.dynamic_slice_in_dim(narrow, (1 - me) * share, share, 2)
        total = add(mine, shift(theirs, "col", 1))
    else:
        total = lax.psum_scatter(narrow, "col", scatter_dimension=2, tiled=True)
    total = exchange_sum(total, "pole")
    return exchange_sum(total, "row").astype(F32)


def body(
    inverse_front, tile_mask, lower_panel, upper_panel, pivots, pole_weight, pole_slot, supernode
):
    front = inverse_front[0]
    _, rows, _ = front.shape
    width = pivots.shape[2]
    tile = rows // tile_mask.shape[0]
    me = lax.axis_index("row")
    order = jnp.arange(PIECES, dtype=jnp.int32)
    if lax.axis_size("row") == 4:
        order = jnp.stack([me ^ 1, me ^ 3, me ^ 2, me]).astype(jnp.int32)
    unit = rows // 4 if rows % (4 * tile) == 0 else rows
    parts = {panel: [(a * unit, b * unit) for a, b in PARTS[panel]] for panel in range(2)}
    if unit == rows:
        parts = {panel: [(0, rows)] for panel in range(2)}
    row = lax.axis_index("row")
    inner = ((row > 0) & (row < lax.axis_size("row") - 1)).astype(jnp.int32)[None]
    mine = lax.dynamic_index_in_dim(pole_slot, lax.axis_index("pole"), 0, keepdims=False)
    weight = jnp.sum(
        jnp.where(
            jnp.arange(pole_weight.shape[1], dtype=jnp.int32)[None, :] == mine, pole_weight, 0.0
        ),
        axis=1,
    )

    def x_phase(front, slots, panel):
        terms = [
            x_part(front, tile_mask, row_owners, inner, slots, *at, tile)
            for at in parts[panel]
        ]
        pairs = [terms_over_col(x) for x in terms]
        scaled = [scale(one, two, pivots[panel, 0][None, :]) for one, two in pairs]
        return terms, scaled

    row_owners, lower0 = gather_line(lower_panel[0, 0], "row")
    col_owners, upper0 = gather(upper_panel[0, 0], "col")
    _, upper1 = gather(upper_panel[1, 0], "col")
    _, lower1 = gather_line(lower_panel[1, 0], "row")
    y_terms = y_parts(front, tile_mask, order, flat(upper0[:1]), tile)
    y_terms += y_parts(front, tile_mask, order, flat(upper0[1:]), tile)
    y_sums = sum_first(y_terms)
    terms0, scaled = x_phase(front, lower0, 0)

    target = None
    y_terms = [None] * PIECES
    for k in UPDATES:
        target, y_terms[k] = update_y(
            front, target, tile_mask, col_owners, inner, order, scaled,
            y_sums[k], upper1, k, tile,
        )
    y_sums = sum_next(y_terms)
    terms1, scaled = x_phase(target, lower1, 1)
    raw0 = density_part(terms0, col_owners, inner, upper0, weight)
    raw1 = density_part(terms1, col_owners, inner, upper1, weight)
    raw = reduce_density(jnp.stack([raw0, raw1]))
    for k in LAST_UPDATES:
        target = update(target, tile_mask, order, scaled, y_sums[k], k, tile)

    share = width // lax.axis_size("col")
    col_start = lax.axis_index("col") * share
    results = []
    for panel in range(2):
        labels_rows = lax.dynamic_slice_in_dim(supernode, panel * width, width)
        labels_cols = lax.dynamic_slice_in_dim(supernode, panel * width + col_start, share)
        same_node = labels_rows[:, None] == labels_cols[None, :]
        results.append(jnp.where(same_node, raw[panel], jnp.zeros((), F32)))
    return target[None], jnp.stack(results)


PIECES = 4
UPDATES = (3, 0, 2, 1)
LAST_UPDATES = (3, 0, 2, 1)
PARTS = (((0, 2), (2, 2)), ((0, 2), (2, 1), (3, 1)))


def solution(mesh):
    in_specs = (
        P(("grp", "pole"), None, "row", "col"),
        P(("grp", "row"), "col"),
        P(None, ("grp", "pole"), None, "row", "col"),
        P(None, ("grp", "pole"), None, "col", "row"),
        P(None, ("grp", "pole"), None),
        P(None, "grp"),
        P("grp"),
        P("grp"),
    )
    out_specs = (P(("grp", "pole"), None, "row", "col"), P("grp", None, "col"))

    return jax.shard_map(body, mesh=mesh, in_specs=in_specs, out_specs=out_specs, check_vma=False)
```

profile of v0, /device:TPU:0, one launch (start us, length us, event | category | flops | bytes accessed | tf_op | source)
XLA Modules:
  0.0 349.5 jit_solution(10188781055447015207)
XLA Ops:
  9.5 13.2 %shard_map.95 = (bf16[2,2,128,512]{3,2,1,0:T(8,128)(2,1)}, bf16[2,2,128,512]{3,2,1,0:T(8,128)(2,1)S(1)}) custom-call(s32[16,16]{1,0:T(8,128)S(1)} %copy-done.4, s32[4]{0:T(128)S(1)} %pad_add_fusion.order, bf16[2,2048,2048]{2,1,0:T(8,128)(2,1)} %bitcast.29, bf16[2,128,2048]{2,1,0:T(8,128)(2,1)S(1)} %get-tuple-element.27.rest_0_.rest_2_), custom_call_target="tpu_custom_call" | custom-call | flops 4294967296 | bytes 18874368 | tf_op jit(solution)/shard_map/pallas_call | solution.py:28
  28.8 13.3 %shard_map.96 = (bf16[2,2,128,512]{3,2,1,0:T(8,128)(2,1)}, bf16[2,2,128,512]{3,2,1,0:T(8,128)(2,1)S(1)}) custom-call(s32[16,16]{1,0:T(8,128)S(1)} %copy-done.4, s32[4]{0:T(128)S(1)} %pad_add_fusion.order, bf16[2,2048,2048]{2,1,0:T(8,128)(2,1)} %bitcast.30, bf16[2,128,2048]{2,1,0:T(8,128)(2,1)} %collective-permute-done.1.rest_0_.rest_3_), custom_call_target="tpu_custom_call" | custom-call | flops 4294967296 | bytes 18874368 | tf_op jit(solution)/shard_map/pallas_call | solution.py:28
  62.0 29.6 %collective-permute-done.8.rest_3_ = bf16[2,64,2048]{2,1,0:T(8,128)(2,1)S(1)} collective-permute-done((bf16[2,64,2048]{2,1,0:T(8,128)(2,1)}, bf16[2,64,2048]{2,1,0:T(8,128)(2,1)S(1)}, u32[]{:S(2)}, u32[]{:S(2)}) %collective-permute-start.8) | collective-permute-done | bytes 524320 | tf_op jit(solution)/shard_map/ppermute | solution.py:392
  91.6 9.5 %collective-permute-done.10.rest_5_ = bf16[2,64,2048]{2,1,0:T(8,128)(2,1)S(1)} collective-permute-done((bf16[2,64,2048]{2,1,0:T(8,128)(2,1)}, bf16[2,64,2048]{2,1,0:T(8,128)(2,1)S(1)}, u32[]{:S(2)}, u32[]{:S(2)}) %collective-permute-start.10) | collective-permute-done | bytes 524320 | tf_op jit(solution)/shard_map/ppermute | solution.py:393
  101.1 8.8 %shard_map.97.rest_0_ = bf16[2,1024,256]{2,1,0:T(8,128)(2,1)S(1)} custom-call(s32[16,16]{1,0:T(8,128)S(1)} %copy-done.4, s32[4]{0:T(128)S(1)} %pad_add_fusion.1.owners, s32[1]{0:T(128)} %bitcast.4.inner, bf16[2,2048,2048]{2,1,0:T(8,128)(2,1)} %bitcast.31, bf16[2,64,2048]{2,1,0:T(8,128)(2,1)} %get-tuple-element.29.rest_0_, ...), custom_call_target="tpu_custom_call" | custom-call | flops 4294967296 | bytes 20971520 | tf_op jit(solution)/shard_map/pallas_call | solution.py:28
  111.5 8.8 %shard_map.98.rest_1_ = bf16[2,1024,256]{2,1,0:T(8,128)(2,1)S(1)} custom-call(s32[16,16]{1,0:T(8,128)S(1)} %copy-done.4, s32[4]{0:T(128)S(1)} %pad_add_fusion.1.owners, s32[1]{0:T(128)} %bitcast.4.inner, bf16[2,2048,2048]{2,1,0:T(8,128)(2,1)} %bitcast.32, bf16[2,64,2048]{2,1,0:T(8,128)(2,1)} %get-tuple-element.29.rest_0_, ...), custom_call_target="tpu_custom_call" | custom-call | flops 4294967296 | bytes 20971520 | tf_op jit(solution)/shard_map/pallas_call | solution.py:28
  137.4 21.2 %collective-permute-done.12 = bf16[2,1024,256]{2,1,0:T(8,128)(2,1)S(1)} collective-permute-done((bf16[2,1024,256]{2,1,0:T(8,128)(2,1)S(1)}, bf16[2,1024,256]{2,1,0:T(8,128)(2,1)S(1)}, u32[]{:S(2)}, u32[]{:S(2)}) %collective-permute-start.12) | collective-permute-done | bytes 1048608 | tf_op jit(solution)/shard_map/ppermute | solution.py:366
  161.3 17.2 %collective-permute-done.14.rest_3_.rest_4_ = bf16[2,128,2048]{2,1,0:T(8,128)(2,1)S(1)} collective-permute-done((bf16[2,128,2048]{2,1,0:T(8,128)(2,1)S(1)}, bf16[2,128,2048]{2,1,0:T(8,128)(2,1)S(1)}, u32[]{:S(2)}, u32[]{:S(2)}) %collective-permute-start.14) | collective-permute-done | bytes 1048608 | tf_op jit(solution)/shard_map/ppermute | solution.py:366
  178.5 8.0 %shard_map.99 = (bf16[2,2048,2048]{2,1,0:T(8,128)(2,1)}, bf16[2,256,512]{2,1,0:T(8,128)(2,1)S(1)}) custom-call(s32[16,16]{1,0:T(8,128)S(1)} %copy-done.4, s32[2]{0:T(128)S(1)} %and_select_fusion.owners, s32[1]{0:T(128)} %bitcast.4.inner, s32[4]{0:T(128)S(1)} %pad_add_fusion.order, bf16[2,2048,2048]{2,1,0:T(8,128)(2,1)} %bitcast.33, ...), custom_call_target="tpu_custom_call" | custom-call | flops 4294967296 | bytes 38797312 | tf_op jit(solution)/shard_map/pallas_call | solution.py:28
  186.5 5.4 %collective-permute-done.13.y = bf16[2,2,128,512]{3,2,1,0:T(8,128)(2,1)S(1)} collective-permute-done((bf16[2,2,128,512]{3,2,1,0:T(8,128)(2,1)S(1)}, bf16[2,2,128,512]{3,2,1,0:T(8,128)(2,1)S(1)}, u32[]{:S(2)}, u32[]{:S(2)}) %collective-permute-start.13) | collective-permute-done | bytes 524320 | tf_op jit(solution)/shard_map/ppermute | solution.py:406
  191.9 7.8 %shard_map.100 = (bf16[2,2048,2048]{2,1,0:T(8,128)(2,1)}, bf16[2,256,512]{2,1,0:T(8,128)(2,1)S(1)}) custom-call(s32[16,16]{1,0:T(8,128)S(1)} %copy-done.4, s32[2]{0:T(128)S(1)} %and_select_fusion.owners, s32[1]{0:T(128)} %bitcast.4.inner, s32[4]{0:T(128)S(1)} %pad_add_fusion.order, bf16[2,2048,2048]{2,1,0:T(8,128)(2,1)} %bitcast.34, ...), custom_call_target="tpu_custom_call", output_to_operand_aliasing={{0}: (8, {})} | custom-call | flops 4294967296 | bytes 55574528 | tf_op jit(solution)/shard_map/pallas_call | solution.py:28
  200.5 7.8 %shard_map.101 = (bf16[2,2048,2048]{2,1,0:T(8,128)(2,1)}, bf16[2,256,512]{2,1,0:T(8,128)(2,1)S(1)}) custom-call(s32[16,16]{1,0:T(8,128)S(1)} %copy-done.4, s32[2]{0:T(128)S(1)} %and_select_fusion.owners, s32[1]{0:T(128)} %bitcast.4.inner, s32[4]{0:T(128)S(1)} %pad_add_fusion.order, bf16[2,2048,2048]{2,1,0:T(8,128)(2,1)} %bitcast.35, ...), custom_call_target="tpu_custom_call", output_to_operand_aliasing={{0}: (8, {})} | custom-call | flops 4294967296 | bytes 55574528 | tf_op jit(solution)/shard_map/pallas_call | solution.py:28
  208.4 7.8 %shard_map.102 = (bf16[2,2048,2048]{2,1,0:T(8,128)(2,1)}, bf16[2,256,512]{2,1,0:T(8,128)(2,1)S(1)}) custom-call(s32[16,16]{1,0:T(8,128)S(1)} %copy-done.4, s32[2]{0:T(128)S(1)} %and_select_fusion.owners, s32[1]{0:T(128)} %bitcast.4.inner, s32[4]{0:T(128)S(1)} %pad_add_fusion.order, bf16[2,2048,2048]{2,1,0:T(8,128)(2,1)} %bitcast.36, ...), custom_call_target="tpu_custom_call", output_to_operand_aliasing={{0}: (8, {})} | custom-call | flops 4294967296 | bytes 55574528 | tf_op jit(solution)/shard_map/pallas_call | solution.py:28
  217.0 5.2 %shard_map.105.rest_2_ = bf16[2,512,256]{2,1,0:T(8,128)(2,1)S(1)} custom-call(s32[16,16]{1,0:T(8,128)S(1)} %copy-done.4, s32[4]{0:T(128)S(1)} %pad_add_fusion.1.owners, s32[1]{0:T(128)} %bitcast.4.inner, bf16[2,2048,2048]{2,1,0:T(8,128)(2,1)} %get-tuple-element.21.front, bf16[2,64,2048]{2,1,0:T(8,128)(2,1)S(1)} %get-tuple-element.28.rest_0_, ...), custom_call_target="tpu_custom_call" | custom-call | flops 2147483648 | bytes 20447232 | tf_op jit(solution)/shard_map/pallas_call | solution.py:28
  222.2 5.4 %shard_map.104.rest_1_ = bf16[2,512,256]{2,1,0:T(8,128)(2,1)S(1)} custom-call(s32[16,16]{1,0:T(8,128)S(1)} %copy-done.4, s32[4]{0:T(128)S(1)} %pad_add_fusion.1.owners, s32[1]{0:T(128)} %bitcast.4.inner, bf16[2,2048,2048]{2,1,0:T(8,128)(2,1)} %get-tuple-element.21.front, bf16[2,64,2048]{2,1,0:T(8,128)(2,1)S(1)} %get-tuple-element.28.rest_0_, ...), custom_call_target="tpu_custom_call" | custom-call | flops 2147483648 | bytes 20447232 | tf_op jit(solution)/shard_map/pallas_call | solution.py:28
  227.6 8.2 %shard_map.103.rest_0_ = bf16[2,1024,256]{2,1,0:T(8,128)(2,1)S(1)} custom-call(s32[16,16]{1,0:T(8,128)S(1)} %copy-done.4, s32[4]{0:T(128)S(1)} %pad_add_fusion.1.owners, s32[1]{0:T(128)} %bitcast.4.inner, bf16[2,2048,2048]{2,1,0:T(8,128)(2,1)} %get-tuple-element.21.front, bf16[2,64,2048]{2,1,0:T(8,128)(2,1)S(1)} %get-tuple-element.28.rest_0_, ...), custom_call_target="tpu_custom_call" | custom-call | flops 4294967296 | bytes 20971520 | tf_op jit(solution)/shard_map/pallas_call | solution.py:28
  248.6 12.3 %collective-permute-done.31 = bf16[2,256,128]{2,1,0:T(8,128)(2,1)S(1)} collective-permute-done((bf16[2,256,128]{2,1,0:T(8,128)(2,1)S(1)}, bf16[2,256,128]{2,1,0:T(8,128)(2,1)S(1)}, u32[]{:S(2)}, u32[]{:S(2)}) %collective-permute-start.31) | collective-permute-done | bytes 131104 | tf_op jit(solution)/shard_map/ppermute | solution.py:459
  263.8 8.3 %collective-permute-done.32 = bf16[2,256,128]{2,1,0:T(8,128)(2,1)S(1)} collective-permute-done((bf16[2,256,128]{2,1,0:T(8,128)(2,1)S(1)}, bf16[2,256,128]{2,1,0:T(8,128)(2,1)S(1)}, u32[]{:S(2)}, u32[]{:S(2)}) %collective-permute-start.32) | collective-permute-done | bytes 131104 | tf_op jit(solution)/shard_map/ppermute | solution.py:459
  276.0 22.7 %collective-permute-done.17 = bf16[2,256,512]{2,1,0:T(8,128)(2,1)S(1)} collective-permute-done((bf16[2,256,512]{2,1,0:T(8,128)(2,1)S(1)}, bf16[2,256,512]{2,1,0:T(8,128)(2,1)S(1)}, u32[]{:S(2)}, u32[]{:S(2)}) %collective-permute-start.17) | collective-permute-done | bytes 524320 | tf_op jit(solution)/shard_map/ppermute | solution.py:406
  303.5 20.9 %collective-permute-done.27.y = bf16[2,256,512]{2,1,0:T(8,128)(2,1)S(1)} collective-permute-done((bf16[2,256,512]{2,1,0:T(8,128)(2,1)S(1)}, bf16[2,256,512]{2,1,0:T(8,128)(2,1)S(1)}, u32[]{:S(2)}, u32[]{:S(2)}) %collective-permute-start.27) | collective-permute-done | bytes 524320 | tf_op jit(solution)/shard_map/ppermute | solution.py:406
  324.4 6.3 %shard_map.106.front = bf16[2,2048,2048]{2,1,0:T(8,128)(2,1)} custom-call(s32[16,16]{1,0:T(8,128)S(1)} %copy-done.4, s32[4]{0:T(128)S(1)} %pad_add_fusion.order, bf16[2,2048,2048]{2,1,0:T(8,128)(2,1)} %get-tuple-element.21.front, bf16[2,256,512]{2,1,0:T(8,128)(2,1)S(1)} %add_convert_fusion.5.y, ...), custom_call_target="tpu_custom_call", output_to_operand_aliasing={{}: (2, {})} | custom-call | flops 2147483648 | bytes 36175872 | tf_op jit(solution)/shard_map/pallas_call | solution.py:28
  330.6 6.3 %shard_map.107.front = bf16[2,2048,2048]{2,1,0:T(8,128)(2,1)} custom-call(s32[16,16]{1,0:T(8,128)S(1)} %copy-done.4, s32[4]{0:T(128)S(1)} %pad_add_fusion.order, bf16[2,2048,2048]{2,1,0:T(8,128)(2,1)} %shard_map.106.front, bf16[2,256,512]{2,1,0:T(8,128)(2,1)S(1)} %collective-permute-done.26.y, ...), custom_call_target="tpu_custom_call", output_to_operand_aliasing={{}: (2, {})} | custom-call | flops 2147483648 | bytes 36175872 | tf_op jit(solution)/shard_map/pallas_call | solution.py:28
  336.9 6.3 %shard_map.108.front = bf16[2,2048,2048]{2,1,0:T(8,128)(2,1)} custom-call(s32[16,16]{1,0:T(8,128)S(1)} %copy-done.4, s32[4]{0:T(128)S(1)} %pad_add_fusion.order, bf16[2,2048,2048]{2,1,0:T(8,128)(2,1)} %shard_map.107.front, bf16[2,256,512]{2,1,0:T(8,128)(2,1)S(1)} %collective-permute-done.27.y, ...), custom_call_target="tpu_custom_call", output_to_operand_aliasing={{}: (2, {})} | custom-call | flops 2147483648 | bytes 36175872 | tf_op jit(solution)/shard_map/pallas_call | solution.py:28
  343.2 6.3 %shard_map.109 = bf16[2,2048,2048]{2,1,0:T(8,128)(2,1)} custom-call(s32[16,16]{1,0:T(8,128)S(1)} %copy-done.4, s32[4]{0:T(128)S(1)} %pad_add_fusion.order, bf16[2,2048,2048]{2,1,0:T(8,128)(2,1)} %shard_map.108.front, bf16[2,256,512]{2,1,0:T(8,128)(2,1)S(1)} %collective-permute-done.28.y, ...), custom_call_target="tpu_custom_call", output_to_operand_aliasing={{}: (2, {})} | custom-call | flops 2147483648 | bytes 36175872 | tf_op jit(solution)/shard_map/pallas_call | solution.py:28
  (127 shorter events, 81.7 us)
Async XLA Ops:
  2.5 26.3 %collective-permute-start.1 = (bf16[2,128,2048]{2,1,0:T(8,128)(2,1)S(1)}, bf16[2,128,2048]{2,1,0:T(8,128)(2,1)}, u32[]{:S(2)}, u32[]{:S(2)}) collective-permute-start(bf16[2,128,2048]{2,1,0:T(8,128)(2,1)S(1)} %get-tuple-element.27.rest_0_.rest_2_), channel_id=1, source_target_pairs={{0,2},{2,0},{1,3},{3,1},{4,6},{6,4},{5,7},{7,5},{8,10},{10,8},{9,1... | collective-permute-start | bytes 3145736 | tf_op jit(solution)/shard_map/ppermute | solution.py:366
  7.9 38.1 %collective-permute-start.7 = (bf16[2,64,2048]{2,1,0:T(8,128)(2,1)}, bf16[2,64,2048]{2,1,0:T(8,128)(2,1)}, u32[]{:S(2)}, u32[]{:S(2)}) collective-permute-start(bf16[2,64,2048]{2,1,0:T(8,128)(2,1)} %get-tuple-element.29.rest_0_), channel_id=1, source_target_pairs={{4,8},{8,4},{5,9},{9,5},{6,10},{10,6},{7,11},{11,7},{20,24},{24,20... | collective-permute-start | bytes 1572872 | tf_op jit(solution)/shard_map/ppermute | solution.py:390
  23.4 27.1 %collective-permute-start = (bf16[2,2,128,512]{3,2,1,0:T(8,128)(2,1)}, bf16[2,2,128,512]{3,2,1,0:T(8,128)(2,1)}, u32[]{:S(2)}, u32[]{:S(2)}) collective-permute-start(bf16[2,2,128,512]{3,2,1,0:T(8,128)(2,1)} %get-tuple-element.15), channel_id=1, source_target_pairs={{0,4},{4,0},{8,12},{12,8},{1,5},{5,1},{9,13},{13,9},{2,6},{6,2},{1... | collective-permute-start | bytes 1572872 | tf_op jit(solution)/shard_map/ppermute | solution.py:406
  27.1 24.7 %collective-permute-start.9 = (bf16[2,64,2048]{2,1,0:T(8,128)(2,1)}, bf16[2,64,2048]{2,1,0:T(8,128)(2,1)}, u32[]{:S(2)}, u32[]{:S(2)}) collective-permute-start(bf16[2,64,2048]{2,1,0:T(8,128)(2,1)} %collective-permute-done.6.rest_1_), channel_id=1, source_target_pairs={{4,8},{8,4},{5,9},{9,5},{6,10},{10,6},{7,11},{11,7},{20,24},{24,20... | collective-permute-start | bytes 1572872 | tf_op jit(solution)/shard_map/ppermute | solution.py:391
  44.7 79.9 %collective-permute-start.19 = (bf16[2,64,2048]{2,1,0:T(8,128)(2,1)S(1)}, bf16[2,64,2048]{2,1,0:T(8,128)(2,1)S(1)}, u32[]{:S(2)}, u32[]{:S(2)}) collective-permute-start(bf16[2,64,2048]{2,1,0:T(8,128)(2,1)S(1)} %get-tuple-element.28.rest_0_), channel_id=1, source_target_pairs={{4,8},{8,4},{5,9},{9,5},{6,10},{10,6},{7,11},{11,7},{20,24},{24,20... | collective-permute-start | bytes 1572872 | tf_op jit(solution)/shard_map/ppermute | solution.py:390
  46.1 74.9 %collective-permute-start.18 = (bf16[2,64,2048]{2,1,0:T(8,128)(2,1)S(1)}, bf16[2,64,2048]{2,1,0:T(8,128)(2,1)S(1)}, u32[]{:S(2)}, u32[]{:S(2)}) collective-permute-start(bf16[2,64,2048]{2,1,0:T(8,128)(2,1)S(1)} %get-tuple-element.28.rest_0_), channel_id=1, source_target_pairs={{0,4},{4,0},{8,12},{12,8},{1,5},{5,1},{9,13},{13,9},{2,6},{6,2},{1... | collective-permute-start | bytes 1572872 | tf_op jit(solution)/shard_map/ppermute | solution.py:389
  50.5 41.1 %collective-permute-start.8 = (bf16[2,64,2048]{2,1,0:T(8,128)(2,1)}, bf16[2,64,2048]{2,1,0:T(8,128)(2,1)S(1)}, u32[]{:S(2)}, u32[]{:S(2)}) collective-permute-start(bf16[2,64,2048]{2,1,0:T(8,128)(2,1)} %collective-permute-done.7.rest_2_), channel_id=1, source_target_pairs={{4,0},{8,12},{5,1},{9,13},{6,2},{10,14},{7,3},{11,15},{20,16},{24,... | collective-permute-start | bytes 1572872 | tf_op jit(solution)/shard_map/ppermute | solution.py:392
  51.8 49.3 %collective-permute-start.10 = (bf16[2,64,2048]{2,1,0:T(8,128)(2,1)}, bf16[2,64,2048]{2,1,0:T(8,128)(2,1)S(1)}, u32[]{:S(2)}, u32[]{:S(2)}) collective-permute-start(bf16[2,64,2048]{2,1,0:T(8,128)(2,1)} %collective-permute-done.9.rest_4_), channel_id=1, source_target_pairs={{4,0},{8,12},{5,1},{9,13},{6,2},{10,14},{7,3},{11,15},{20,16},{24,... | collective-permute-start | bytes 1572872 | tf_op jit(solution)/shard_map/ppermute | solution.py:393
  59.1 63.4 %collective-permute-start.3 = (bf16[2,2,128,512]{3,2,1,0:T(8,128)(2,1)S(1)}, bf16[2,2,128,512]{3,2,1,0:T(8,128)(2,1)S(1)}, u32[]{:S(2)}, u32[]{:S(2)}) collective-permute-start(bf16[2,2,128,512]{3,2,1,0:T(8,128)(2,1)S(1)} %pad_maximum_fusion), channel_id=1, source_target_pairs={{0,8},{4,12},{8,0},{12,4},{1,9},{5,13},{9,1},{13,5},{2,10},{6,14},... | collective-permute-start | bytes 1572872 | tf_op jit(solution)/shard_map/ppermute | solution.py:406
  110.0 26.1 %collective-permute-start.11 = (bf16[2,1024,256]{2,1,0:T(8,128)(2,1)S(1)}, bf16[2,1024,256]{2,1,0:T(8,128)(2,1)S(1)}, u32[]{:S(2)}, u32[]{:S(2)}) collective-permute-start(bf16[2,1024,256]{2,1,0:T(8,128)(2,1)S(1)} %shard_map.97.rest_0_), channel_id=1, source_target_pairs={{0,2},{2,0},{1,3},{3,1},{4,6},{6,4},{5,7},{7,5},{8,10},{10,8},{9,1... | collective-permute-start | bytes 3145736 | tf_op jit(solution)/shard_map/ppermute | solution.py:366
  120.4 38.2 %collective-permute-start.12 = (bf16[2,1024,256]{2,1,0:T(8,128)(2,1)S(1)}, bf16[2,1024,256]{2,1,0:T(8,128)(2,1)S(1)}, u32[]{:S(2)}, u32[]{:S(2)}) collective-permute-start(bf16[2,1024,256]{2,1,0:T(8,128)(2,1)S(1)} %shard_map.98.rest_1_), channel_id=1, source_target_pairs={{0,2},{2,0},{1,3},{3,1},{4,6},{6,4},{5,7},{7,5},{8,10},{10,8},{9,1... | collective-permute-start | bytes 3145736 | tf_op jit(solution)/shard_map/ppermute | solution.py:366
  121.0 57.4 %collective-permute-start.14 = (bf16[2,128,2048]{2,1,0:T(8,128)(2,1)S(1)}, bf16[2,128,2048]{2,1,0:T(8,128)(2,1)S(1)}, u32[]{:S(2)}, u32[]{:S(2)}) collective-permute-start(bf16[2,128,2048]{2,1,0:T(8,128)(2,1)S(1)} %get-tuple-element.26.rest_2_.rest_3_), channel_id=1, source_target_pairs={{0,2},{2,0},{1,3},{3,1},{4,6},{6,4},{5,7},{7,5},{8,10},{10,8},{9,1... | collective-permute-start | bytes 3145736 | tf_op jit(solution)/shard_map/ppermute | solution.py:366
  124.6 34.0 %collective-permute-start.4 = (bf16[2,2,128,512]{3,2,1,0:T(8,128)(2,1)S(1)}, bf16[2,2,128,512]{3,2,1,0:T(8,128)(2,1)S(1)}, u32[]{:S(2)}, u32[]{:S(2)}) collective-permute-start(bf16[2,2,128,512]{3,2,1,0:T(8,128)(2,1)S(1)} %pad_maximum_fusion.1.y), channel_id=1, source_target_pairs={{0,8},{4,12},{8,0},{12,4},{1,9},{5,13},{9,1},{13,5},{2,10},{6,14},... | collective-permute-start | bytes 1572872 | tf_op jit(solution)/shard_map/ppermute | solution.py:406
  131.6 85.4 %collective-permute-start.20 = (bf16[2,64,2048]{2,1,0:T(8,128)(2,1)S(1)}, bf16[2,64,2048]{2,1,0:T(8,128)(2,1)S(1)}, u32[]{:S(2)}, u32[]{:S(2)}) collective-permute-start(bf16[2,64,2048]{2,1,0:T(8,128)(2,1)S(1)} %collective-permute-done.19.rest_2_), channel_id=1, source_target_pairs={{4,0},{8,12},{5,1},{9,13},{6,2},{10,14},{7,3},{11,15},{20,16},{24,... | collective-permute-start | bytes 1572872 | tf_op jit(solution)/shard_map/ppermute | solution.py:392
  136.1 80.9 %collective-permute-start.22 = (bf16[2,64,2048]{2,1,0:T(8,128)(2,1)S(1)}, bf16[2,64,2048]{2,1,0:T(8,128)(2,1)S(1)}, u32[]{:S(2)}, u32[]{:S(2)}) collective-permute-start(bf16[2,64,2048]{2,1,0:T(8,128)(2,1)S(1)} %collective-permute-done.21.rest_4_), channel_id=1, source_target_pairs={{4,0},{8,12},{5,1},{9,13},{6,2},{10,14},{7,3},{11,15},{20,16},{24,... | collective-permute-start | bytes 1572872 | tf_op jit(solution)/shard_map/ppermute | solution.py:393
  158.6 33.3 %collective-permute-start.13 = (bf16[2,2,128,512]{3,2,1,0:T(8,128)(2,1)S(1)}, bf16[2,2,128,512]{3,2,1,0:T(8,128)(2,1)S(1)}, u32[]{:S(2)}, u32[]{:S(2)}) collective-permute-start(bf16[2,2,128,512]{3,2,1,0:T(8,128)(2,1)S(1)} %pad_maximum_fusion.1.y), channel_id=1, source_target_pairs={{0,4},{4,0},{8,12},{12,8},{1,5},{5,1},{9,13},{13,9},{2,6},{6,2},{1... | collective-permute-start | bytes 1572872 | tf_op jit(solution)/shard_map/ppermute | solution.py:406
  158.6 49.8 %collective-permute-start.5 = (bf16[2,2,128,512]{3,2,1,0:T(8,128)(2,1)S(1)}, bf16[2,2,128,512]{3,2,1,0:T(8,128)(2,1)S(1)}, u32[]{:S(2)}, u32[]{:S(2)}) collective-permute-start(bf16[2,2,128,512]{3,2,1,0:T(8,128)(2,1)S(1)} %collective-permute-done.4.y), channel_id=1, source_target_pairs={{0,4},{4,0},{8,12},{12,8},{1,5},{5,1},{9,13},{13,9},{2,6},{6,2},{1... | collective-permute-start | bytes 1572872 | tf_op jit(solution)/shard_map/ppermute | solution.py:406
  245.3 30.7 %collective-permute-start.15 = (bf16[2,256,512]{2,1,0:T(8,128)(2,1)}, bf16[2,256,512]{2,1,0:T(8,128)(2,1)S(1)}, u32[]{:S(2)}, u32[]{:S(2)}) collective-permute-start(bf16[2,256,512]{2,1,0:T(8,128)(2,1)} %copy-done.13), channel_id=1, source_target_pairs={{0,4},{4,0},{8,12},{12,8},{1,5},{5,1},{9,13},{13,9},{2,6},{6,2},{1... | collective-permute-start | bytes 1572872 | tf_op jit(solution)/shard_map/ppermute | solution.py:406
  246.6 29.0 %collective-permute-start.24 = (bf16[2,512,256]{2,1,0:T(8,128)(2,1)}, bf16[2,512,256]{2,1,0:T(8,128)(2,1)S(1)}, u32[]{:S(2)}, u32[]{:S(2)}) collective-permute-start(bf16[2,512,256]{2,1,0:T(8,128)(2,1)} %copy-done.2), channel_id=1, source_target_pairs={{0,2},{2,0},{1,3},{3,1},{4,6},{6,4},{5,7},{7,5},{8,10},{10,8},{9,1... | collective-permute-start | bytes 1572872 | tf_op jit(solution)/shard_map/ppermute | solution.py:366
  247.1 28.6 %collective-permute-start.25 = (bf16[2,512,256]{2,1,0:T(8,128)(2,1)}, bf16[2,512,256]{2,1,0:T(8,128)(2,1)S(1)}, u32[]{:S(2)}, u32[]{:S(2)}) collective-permute-start(bf16[2,512,256]{2,1,0:T(8,128)(2,1)} %copy-done), channel_id=1, source_target_pairs={{0,2},{2,0},{1,3},{3,1},{4,6},{6,4},{5,7},{7,5},{8,10},{10,8},{9,1... | collective-permute-start | bytes 1572872 | tf_op jit(solution)/shard_map/ppermute | solution.py:366
  260.9 42.3 %collective-permute-start.23 = (bf16[2,1024,256]{2,1,0:T(8,128)(2,1)S(1)}, bf16[2,1024,256]{2,1,0:T(8,128)(2,1)S(1)}, u32[]{:S(2)}, u32[]{:S(2)}) collective-permute-start(bf16[2,1024,256]{2,1,0:T(8,128)(2,1)S(1)} %shard_map.103.rest_0_), channel_id=1, source_target_pairs={{0,2},{2,0},{1,3},{3,1},{4,6},{6,4},{5,7},{7,5},{8,10},{10,8},{9,1... | collective-permute-start | bytes 3145736 | tf_op jit(solution)/shard_map/ppermute | solution.py:366
  272.2 26.6 %collective-permute-start.17 = (bf16[2,256,512]{2,1,0:T(8,128)(2,1)S(1)}, bf16[2,256,512]{2,1,0:T(8,128)(2,1)S(1)}, u32[]{:S(2)}, u32[]{:S(2)}) collective-permute-start(bf16[2,256,512]{2,1,0:T(8,128)(2,1)S(1)} %add_convert_fusion.6), channel_id=1, source_target_pairs={{0,8},{4,12},{8,0},{12,4},{1,9},{5,13},{9,1},{13,5},{2,10},{6,14},... | collective-permute-start | bytes 1572872 | tf_op jit(solution)/shard_map/ppermute | solution.py:406
  299.0 25.4 %collective-permute-start.27 = (bf16[2,256,512]{2,1,0:T(8,128)(2,1)S(1)}, bf16[2,256,512]{2,1,0:T(8,128)(2,1)S(1)}, u32[]{:S(2)}, u32[]{:S(2)}) collective-permute-start(bf16[2,256,512]{2,1,0:T(8,128)(2,1)S(1)} %add_convert_fusion.5.y), channel_id=1, source_target_pairs={{0,8},{4,12},{8,0},{12,4},{1,9},{5,13},{9,1},{13,5},{2,10},{6,14},... | collective-permute-start | bytes 1572872 | tf_op jit(solution)/shard_map/ppermute | solution.py:406
  299.2 31.5 %collective-permute-start.26 = (bf16[2,256,512]{2,1,0:T(8,128)(2,1)S(1)}, bf16[2,256,512]{2,1,0:T(8,128)(2,1)S(1)}, u32[]{:S(2)}, u32[]{:S(2)}) collective-permute-start(bf16[2,256,512]{2,1,0:T(8,128)(2,1)S(1)} %add_convert_fusion.5.y), channel_id=1, source_target_pairs={{0,4},{4,0},{8,12},{12,8},{1,5},{5,1},{9,13},{13,9},{2,6},{6,2},{1... | collective-permute-start | bytes 1572872 | tf_op jit(solution)/shard_map/ppermute | solution.py:406
  (29 other events, 383.2 us)
where the time goes:
time: 350 us; the launch traced here: 349 us
  waiting for transfers between devices  160 us (46%)
  Pallas kernels  125 us (36%)
  starting transfers between devices  48.8 us (14%)
  other arithmetic  8.2 us (2%)
  local copies, waits for them, and re-layouts  6.63 us (2%)
    pallas_call x17, Pallas kernels, call(): pl.pallas_call(kernel, grid_spec=pltpu.PrefetchScalarGridSpec(num_scalar_...  125 us
    ppermute x12, waiting for transfers between devices, flip(): return lax.ppermute(value, 'row', pairs)  52.8 us
    ppermute x8, waiting for transfers between devices, shift(): return lax.ppermute(value, axis, [(i, (i + by) % n) for i in range(n)])  46.3 us
    ppermute x2, waiting for transfers between devices, gather_line(): out0 = lax.ppermute(mid0, axis, outward)  29.6 us
    ppermute x3, waiting for transfers between devices, exchange_sum(): other = lax.ppermute(value, axis, partner)  21.9 us
    ppermute x12, starting transfers between devices, flip(): return lax.ppermute(value, 'row', pairs)  21.5 us
    ppermute x8, starting transfers between devices, shift(): return lax.ppermute(value, axis, [(i, (i + by) % n) for i in range(n)])  9.77 us
    ppermute x2, waiting for transfers between devices, gather_line(): out1 = lax.ppermute(mid1, axis, outward)  9.54 us
  transfers between devices with their start and end apart: 33, of which 14 were waited for; matrix products, arithmetic and copies ran while one was open for 3% of the time, Pallas kernels for 28%

commit v1 on v0

--- a/solution.py
+++ b/solution.py
@@ -97,48 +97,41 @@
     )
 
 
-def y_kernel(mask, order, front, *rest, tile, count):
-    slots, (*outs, masked) = rest[:count], rest[count:]
+def y_kernel(mask, order, front, *rest, tile, half):
+    *slots_outs, masked = rest
+    count = len(slots_outs) // 2
+    slots, outs = slots_outs[:count], slots_outs[count:]
+    per_piece = pl.num_programs(0) // 2
     step = pl.program_id(0)
-    per_piece = pl.num_programs(0) // PIECES
-    block = order[step // per_piece] * per_piece + step % per_piece
+    block = order[2 * half + step // per_piece] * per_piece + step % per_piece
     masked_tiles(mask, front, masked, tile, 0, block * (front.shape[2] // tile))
-    for s, slot in enumerate(slots):
+    for slot, y_ref in zip(slots, outs):
         upper = slot[...].reshape(2 * slot.shape[1], slot.shape[2])
-        y = negative_product(upper, masked)
-        for k in range(2):
-
-            @pl.when(step // (2 * per_piece) == k)
-            def _(y_ref=outs[2 * s + k], y=y):
-                y_ref[0, 0], y_ref[0, 1] = y
-
-
-def y_parts(front, mask, order, slots, tile):
+        y_ref[0, 0], y_ref[0, 1] = negative_product(upper, masked)
+
+
+def y_part(front, mask, order, slots, half, tile):
     _, rows, cols = front.shape
     share = slots[0].shape[1]
     span = cols // PIECES
     block = min(256, span)
     per_piece = span // block
 
-    def out_spec(k):
-        def place(j, *_):
-            at = jnp.clip(j - 2 * k * per_piece, 0, 2 * per_piece - 1)
-            return (at // per_piece, 0, 0, at % per_piece)
-
-        return pl.BlockSpec((1, 2, share, block), place)
-
     def column(j, mask, order):
-        return (0, 0, order[j // per_piece] * per_piece + j % per_piece)
-
-    outs = [(jax.ShapeDtypeStruct((2, 2, share, span), BF16), out_spec(k)) for k in range(2)]
+        return (0, 0, order[2 * half + j // per_piece] * per_piece + j % per_piece)
+
+    out = (
+        jax.ShapeDtypeStruct((2, 2, share, span), BF16),
+        pl.BlockSpec((1, 2, share, block), lambda j, *_: (j // per_piece, 0, 0, j % per_piece)),
+    )
     return call(
-        functools.partial(y_kernel, tile=tile, count=len(slots)),
-        (cols // block,),
+        functools.partial(y_kernel, tile=tile, half=half),
+        (2 * per_piece,),
         (mask, order),
         [(front, pl.BlockSpec((2, rows, block), column))] + [(s, whole(s.shape)) for s in slots],
-        outs * len(slots),
+        [out] * len(slots),
         [pltpu.VMEM((2, rows, block), BF16)],
-        8 * share * len(slots) * rows * cols,
+        4 * share * len(slots) * rows * cols,
     )
 
 
@@ -420,8 +413,7 @@
     return [near, flip(far, 1), far, own]
 
 
-def sum_first(terms):
-    sent, kept = terms[0::2], terms[1::2]
+def sum_first(sent, kept):
     if lax.axis_size("row") != 4:
         sums = [lax.psum(jnp.concatenate(pair), "row") for pair in zip(sent, kept)]
         return [jnp.stack([total[k] for total in sums]) for k in range(PIECES)]
@@ -515,9 +507,13 @@
     col_owners, upper0 = gather(upper_panel[0, 0], "col")
     _, upper1 = gather(upper_panel[1, 0], "col")
     _, lower1 = gather_line(lower_panel[1, 0], "row")
-    y_terms = y_parts(front, tile_mask, order, flat(upper0[:1]), tile)
-    y_terms += y_parts(front, tile_mask, order, flat(upper0[1:]), tile)
-    y_sums = sum_first(y_terms)
+    halves = []
+    for half in range(2):
+        terms = []
+        for slots in (upper0[:1], upper0[1:]):
+            terms += y_part(front, tile_mask, order, flat(slots), half, tile)
+        halves.append(terms)
+    y_sums = sum_first(*halves)
     terms0, scaled = x_phase(front, lower0, 0)
 
     target = None

time: 350 us -> 341 us (0.974)
  starting transfers between devices: 48.8 us -> 41.9 us
    ppermute x12, starting transfers between devices: 21.5 us -> 16.5 us  [flip(): return lax.ppermute(value, 'row', pairs)]
    pallas_call x17 -> x19, Pallas kernels: 125 us -> 125 us  [call(): pl.pallas_call(kernel, grid_spec=pltpu.PrefetchScalarGridSpec(num_scalar_...]
  transfers between devices with their start and end apart: 33 -> 33, of which waited for: 14 -> 13; matrix products, arithmetic and copies ran while one was open for 3% -> 3% of each run, Pallas kernels for 28% -> 29%
where the time goes in v1:
time: 341 us; the launch traced here: 340 us
  waiting for transfers between devices  158 us (46%)
  Pallas kernels  125 us (37%)
  starting transfers between devices  41.9 us (12%)
  local copies, waits for them, and re-layouts  7.77 us (2%)
  other arithmetic  6.99 us (2%)
    pallas_call x19, Pallas kernels, call(): pl.pallas_call(kernel, grid_spec=pltpu.PrefetchScalarGridSpec(num_scalar_...  125 us
    ppermute x12, waiting for transfers between devices, flip(): return lax.ppermute(value, 'row', pairs)  54 us
    ppermute x8, waiting for transfers between devices, shift(): return lax.ppermute(value, axis, [(i, (i + by) % n) for i in range(n)])  47.5 us
    ppermute x2, waiting for transfers between devices, gather_line(): out0 = lax.ppermute(mid0, axis, outward)  27.9 us
    ppermute x3, waiting for transfers between devices, exchange_sum(): other = lax.ppermute(value, axis, partner)  19.6 us
    ppermute x12, starting transfers between devices, flip(): return lax.ppermute(value, 'row', pairs)  16.5 us
    ppermute x8, starting transfers between devices, shift(): return lax.ppermute(value, axis, [(i, (i + by) % n) for i in range(n)])  10.8 us
    ppermute x2, waiting for transfers between devices, gather_line(): out1 = lax.ppermute(mid1, axis, outward)  8.7 us
  transfers between devices with their start and end apart: 33, of which 13 were waited for; matrix products, arithmetic and copies ran while one was open for 3% of the time, Pallas kernels for 29%

profile of v1, /device:TPU:0, one launch (start us, length us, event | category | flops | bytes accessed | tf_op | source)
XLA Modules:
  0.0 340.3 jit_solution(5380355325189853587)
XLA Ops:
  11.7 7.5 %shard_map.96 = bf16[2,2,128,512]{3,2,1,0:T(8,128)(2,1)} custom-call(s32[16,16]{1,0:T(8,128)S(1)} %copy-done, s32[4]{0:T(128)S(1)} %pad_add_fusion.order, bf16[2,2048,2048]{2,1,0:T(8,128)(2,1)} %bitcast.28, bf16[2,128,2048]{2,1,0:T(8,128)(2,1)S(1)} %get-tuple-element.19.rest_0_.rest_2_), custom_call_target="tpu_custom_call" | custom-call | flops 2147483648 | bytes 18350080 | tf_op jit(solution)/shard_map/pallas_call | solution.py:28
  21.4 6.9 %shard_map.95 = bf16[2,2,128,512]{3,2,1,0:T(8,128)(2,1)S(1)} custom-call(s32[16,16]{1,0:T(8,128)S(1)} %copy-done, s32[4]{0:T(128)S(1)} %pad_add_fusion.order, bf16[2,2048,2048]{2,1,0:T(8,128)(2,1)} %bitcast.29, bf16[2,128,2048]{2,1,0:T(8,128)(2,1)S(1)} %get-tuple-element.19.rest_0_.rest_2_), custom_call_target="tpu_custom_call" | custom-call | flops 2147483648 | bytes 18350080 | tf_op jit(solution)/shard_map/pallas_call | solution.py:28
  29.0 6.9 %shard_map.98 = bf16[2,2,128,512]{3,2,1,0:T(8,128)(2,1)S(1)} custom-call(s32[16,16]{1,0:T(8,128)S(1)} %copy-done, s32[4]{0:T(128)S(1)} %pad_add_fusion.order, bf16[2,2048,2048]{2,1,0:T(8,128)(2,1)} %bitcast.30, bf16[2,128,2048]{2,1,0:T(8,128)(2,1)S(1)} %collective-permute-done.1.rest_0_.rest_3_), custom_call_target="tpu_custom_call" | custom-call | flops 2147483648 | bytes 18350080 | tf_op jit(solution)/shard_map/pallas_call | solution.py:28
  45.4 6.8 %shard_map.97 = bf16[2,2,128,512]{3,2,1,0:T(8,128)(2,1)S(1)} custom-call(s32[16,16]{1,0:T(8,128)S(1)} %copy-done, s32[4]{0:T(128)S(1)} %pad_add_fusion.order, bf16[2,2048,2048]{2,1,0:T(8,128)(2,1)} %bitcast.31, bf16[2,128,2048]{2,1,0:T(8,128)(2,1)S(1)} %collective-permute-done.1.rest_0_.rest_3_), custom_call_target="tpu_custom_call" | custom-call | flops 2147483648 | bytes 18350080 | tf_op jit(solution)/shard_map/pallas_call | solution.py:28
  52.2 7.8 %collective-permute-done.2 = bf16[2,2,128,512]{3,2,1,0:T(8,128)(2,1)S(1)} collective-permute-done((bf16[2,2,128,512]{3,2,1,0:T(8,128)(2,1)S(1)}, bf16[2,2,128,512]{3,2,1,0:T(8,128)(2,1)S(1)}, u32[]{:S(2)}, u32[]{:S(2)}) %collective-permute-start.2) | collective-permute-done | bytes 524320 | tf_op jit(solution)/shard_map/ppermute | solution.py:399
  60.2 27.9 %collective-permute-done.8.rest_3_ = bf16[2,64,2048]{2,1,0:T(8,128)(2,1)S(1)} collective-permute-done((bf16[2,64,2048]{2,1,0:T(8,128)(2,1)}, bf16[2,64,2048]{2,1,0:T(8,128)(2,1)S(1)}, u32[]{:S(2)}, u32[]{:S(2)}) %collective-permute-start.8) | collective-permute-done | bytes 524320 | tf_op jit(solution)/shard_map/ppermute | solution.py:385
  88.1 8.7 %collective-permute-done.10.rest_5_ = bf16[2,64,2048]{2,1,0:T(8,128)(2,1)S(1)} collective-permute-done((bf16[2,64,2048]{2,1,0:T(8,128)(2,1)S(1)}, bf16[2,64,2048]{2,1,0:T(8,128)(2,1)S(1)}, u32[]{:S(2)}, u32[]{:S(2)}) %collective-permute-start.10) | collective-permute-done | bytes 524320 | tf_op jit(solution)/shard_map/ppermute | solution.py:386
  96.8 8.6 %shard_map.99.rest_0_ = bf16[2,1024,256]{2,1,0:T(8,128)(2,1)S(1)} custom-call(s32[16,16]{1,0:T(8,128)S(1)} %copy-done, s32[4]{0:T(128)S(1)} %pad_add_fusion.1.owners, s32[1]{0:T(128)} %bitcast.4.inner, bf16[2,2048,2048]{2,1,0:T(8,128)(2,1)} %bitcast.32, bf16[2,64,2048]{2,1,0:T(8,128)(2,1)} %get-tuple-element.21.rest_0_, ...), custom_call_target="tpu_custom_call" | custom-call | flops 4294967296 | bytes 20971520 | tf_op jit(solution)/shard_map/pallas_call | solution.py:28
  106.0 8.6 %shard_map.100.rest_1_ = bf16[2,1024,256]{2,1,0:T(8,128)(2,1)S(1)} custom-call(s32[16,16]{1,0:T(8,128)S(1)} %copy-done, s32[4]{0:T(128)S(1)} %pad_add_fusion.1.owners, s32[1]{0:T(128)} %bitcast.4.inner, bf16[2,2048,2048]{2,1,0:T(8,128)(2,1)} %bitcast.33, bf16[2,64,2048]{2,1,0:T(8,128)(2,1)} %get-tuple-element.21.rest_0_, ...), custom_call_target="tpu_custom_call" | custom-call | flops 4294967296 | bytes 20971520 | tf_op jit(solution)/shard_map/pallas_call | solution.py:28
  125.1 6.5 %collective-permute-done.11 = bf16[2,1024,256]{2,1,0:T(8,128)(2,1)S(1)} collective-permute-done((bf16[2,1024,256]{2,1,0:T(8,128)(2,1)S(1)}, bf16[2,1024,256]{2,1,0:T(8,128)(2,1)S(1)}, u32[]{:S(2)}, u32[]{:S(2)}) %collective-permute-start.11) | collective-permute-done | bytes 1048608 | tf_op jit(solution)/shard_map/ppermute | solution.py:359
  132.8 21.2 %collective-permute-done.12 = bf16[2,1024,256]{2,1,0:T(8,128)(2,1)S(1)} collective-permute-done((bf16[2,1024,256]{2,1,0:T(8,128)(2,1)S(1)}, bf16[2,1024,256]{2,1,0:T(8,128)(2,1)S(1)}, u32[]{:S(2)}, u32[]{:S(2)}) %collective-permute-start.12) | collective-permute-done | bytes 1048608 | tf_op jit(solution)/shard_map/ppermute | solution.py:359
  156.7 16.3 %collective-permute-done.14.rest_3_.rest_4_ = bf16[2,128,2048]{2,1,0:T(8,128)(2,1)S(1)} collective-permute-done((bf16[2,128,2048]{2,1,0:T(8,128)(2,1)S(1)}, bf16[2,128,2048]{2,1,0:T(8,128)(2,1)S(1)}, u32[]{:S(2)}, u32[]{:S(2)}) %collective-permute-start.14) | collective-permute-done | bytes 1048608 | tf_op jit(solution)/shard_map/ppermute | solution.py:359
  173.1 8.0 %shard_map.101 = (bf16[2,2048,2048]{2,1,0:T(8,128)(2,1)}, bf16[2,256,512]{2,1,0:T(8,128)(2,1)S(1)}) custom-call(s32[16,16]{1,0:T(8,128)S(1)} %copy-done, s32[2]{0:T(128)S(1)} %and_select_fusion.owners, s32[1]{0:T(128)} %bitcast.4.inner, s32[4]{0:T(128)S(1)} %pad_add_fusion.order, bf16[2,2048,2048]{2,1,0:T(8,128)(2,1)} %bitcast.34, ...), custom_call_target="tpu_custom_call" | custom-call | flops 4294967296 | bytes 38797312 | tf_op jit(solution)/shard_map/pallas_call | solution.py:28
  184.5 7.8 %shard_map.102 = (bf16[2,2048,2048]{2,1,0:T(8,128)(2,1)}, bf16[2,256,512]{2,1,0:T(8,128)(2,1)S(1)}) custom-call(s32[16,16]{1,0:T(8,128)S(1)} %copy-done, s32[2]{0:T(128)S(1)} %and_select_fusion.owners, s32[1]{0:T(128)} %bitcast.4.inner, s32[4]{0:T(128)S(1)} %pad_add_fusion.order, bf16[2,2048,2048]{2,1,0:T(8,128)(2,1)} %bitcast.35, ...), custom_call_target="tpu_custom_call", output_to_operand_aliasing={{0}: (8, {})} | custom-call | flops 4294967296 | bytes 55574528 | tf_op jit(solution)/shard_map/pallas_call | solution.py:28
  193.1 7.8 %shard_map.103 = (bf16[2,2048,2048]{2,1,0:T(8,128)(2,1)}, bf16[2,256,512]{2,1,0:T(8,128)(2,1)S(1)}) custom-call(s32[16,16]{1,0:T(8,128)S(1)} %copy-done, s32[2]{0:T(128)S(1)} %and_select_fusion.owners, s32[1]{0:T(128)} %bitcast.4.inner, s32[4]{0:T(128)S(1)} %pad_add_fusion.order, bf16[2,2048,2048]{2,1,0:T(8,128)(2,1)} %bitcast.36, ...), custom_call_target="tpu_custom_call", output_to_operand_aliasing={{0}: (8, {})} | custom-call | flops 4294967296 | bytes 55574528 | tf_op jit(solution)/shard_map/pallas_call | solution.py:28
  200.9 7.8 %shard_map.104 = (bf16[2,2048,2048]{2,1,0:T(8,128)(2,1)}, bf16[2,256,512]{2,1,0:T(8,128)(2,1)S(1)}) custom-call(s32[16,16]{1,0:T(8,128)S(1)} %copy-done, s32[2]{0:T(128)S(1)} %and_select_fusion.owners, s32[1]{0:T(128)} %bitcast.4.inner, s32[4]{0:T(128)S(1)} %pad_add_fusion.order, bf16[2,2048,2048]{2,1,0:T(8,128)(2,1)} %bitcast.37, ...), custom_call_target="tpu_custom_call", output_to_operand_aliasing={{0}: (8, {})} | custom-call | flops 4294967296 | bytes 55574528 | tf_op jit(solution)/shard_map/pallas_call | solution.py:28
  220.6 8.4 %shard_map.105.rest_0_ = bf16[2,1024,256]{2,1,0:T(8,128)(2,1)S(1)} custom-call(s32[16,16]{1,0:T(8,128)S(1)} %copy-done, s32[4]{0:T(128)S(1)} %pad_add_fusion.1.owners, s32[1]{0:T(128)} %bitcast.4.inner, bf16[2,2048,2048]{2,1,0:T(8,128)(2,1)} %get-tuple-element.13.front, bf16[2,64,2048]{2,1,0:T(8,128)(2,1)} %get-tuple-element.20.rest_0_, ...), custom_call_target="tpu_custom_call" | custom-call | flops 4294967296 | bytes 20971520 | tf_op jit(solution)/shard_map/pallas_call | solution.py:28
  244.7 9.8 %collective-permute-done.31 = bf16[2,256,128]{2,1,0:T(8,128)(2,1)S(1)} collective-permute-done((bf16[2,256,128]{2,1,0:T(8,128)(2,1)S(1)}, bf16[2,256,128]{2,1,0:T(8,128)(2,1)S(1)}, u32[]{:S(2)}, u32[]{:S(2)}) %collective-permute-start.31) | collective-permute-done | bytes 131104 | tf_op jit(solution)/shard_map/ppermute | solution.py:451
  256.3 9.1 %collective-permute-done.32 = bf16[2,256,128]{2,1,0:T(8,128)(2,1)S(1)} collective-permute-done((bf16[2,256,128]{2,1,0:T(8,128)(2,1)S(1)}, bf16[2,256,128]{2,1,0:T(8,128)(2,1)S(1)}, u32[]{:S(2)}, u32[]{:S(2)}) %collective-permute-start.32) | collective-permute-done | bytes 131104 | tf_op jit(solution)/shard_map/ppermute | solution.py:451
  269.2 22.3 %collective-permute-done.17 = bf16[2,256,512]{2,1,0:T(8,128)(2,1)S(1)} collective-permute-done((bf16[2,256,512]{2,1,0:T(8,128)(2,1)S(1)}, bf16[2,256,512]{2,1,0:T(8,128)(2,1)S(1)}, u32[]{:S(2)}, u32[]{:S(2)}) %collective-permute-start.17) | collective-permute-done | bytes 524320 | tf_op jit(solution)/shard_map/ppermute | solution.py:399
  295.0 20.4 %collective-permute-done.27.y = bf16[2,256,512]{2,1,0:T(8,128)(2,1)S(1)} collective-permute-done((bf16[2,256,512]{2,1,0:T(8,128)(2,1)S(1)}, bf16[2,256,512]{2,1,0:T(8,128)(2,1)S(1)}, u32[]{:S(2)}, u32[]{:S(2)}) %collective-permute-start.27) | collective-permute-done | bytes 524320 | tf_op jit(solution)/shard_map/ppermute | solution.py:399
  315.4 6.2 %shard_map.108.front = bf16[2,2048,2048]{2,1,0:T(8,128)(2,1)} custom-call(s32[16,16]{1,0:T(8,128)S(1)} %copy-done, s32[4]{0:T(128)S(1)} %pad_add_fusion.order, bf16[2,2048,2048]{2,1,0:T(8,128)(2,1)} %get-tuple-element.13.front, bf16[2,256,512]{2,1,0:T(8,128)(2,1)S(1)} %add_convert_fusion.5.y, ...), custom_call_target="tpu_custom_call", output_to_operand_aliasing={{}: (2, {})} | custom-call | flops 2147483648 | bytes 36175872 | tf_op jit(solution)/shard_map/pallas_call | solution.py:28
  321.6 6.2 %shard_map.109.front = bf16[2,2048,2048]{2,1,0:T(8,128)(2,1)} custom-call(s32[16,16]{1,0:T(8,128)S(1)} %copy-done, s32[4]{0:T(128)S(1)} %pad_add_fusion.order, bf16[2,2048,2048]{2,1,0:T(8,128)(2,1)} %shard_map.108.front, bf16[2,256,512]{2,1,0:T(8,128)(2,1)S(1)} %collective-permute-done.26.y, ...), custom_call_target="tpu_custom_call", output_to_operand_aliasing={{}: (2, {})} | custom-call | flops 2147483648 | bytes 36175872 | tf_op jit(solution)/shard_map/pallas_call | solution.py:28
  334.1 6.2 %shard_map.111 = bf16[2,2048,2048]{2,1,0:T(8,128)(2,1)} custom-call(s32[16,16]{1,0:T(8,128)S(1)} %copy-done, s32[4]{0:T(128)S(1)} %pad_add_fusion.order, bf16[2,2048,2048]{2,1,0:T(8,128)(2,1)} %shard_map.110.front, bf16[2,256,512]{2,1,0:T(8,128)(2,1)S(1)} %collective-permute-done.28.y, ...), custom_call_target="tpu_custom_call", output_to_operand_aliasing={{}: (2, {})} | custom-call | flops 2147483648 | bytes 36175872 | tf_op jit(solution)/shard_map/pallas_call | solution.py:28
  (117 shorter events, 85.7 us)
Async XLA Ops:
  2.4 26.6 %collective-permute-start.1 = (bf16[2,128,2048]{2,1,0:T(8,128)(2,1)S(1)}, bf16[2,128,2048]{2,1,0:T(8,128)(2,1)S(1)}, u32[]{:S(2)}, u32[]{:S(2)}) collective-permute-start(bf16[2,128,2048]{2,1,0:T(8,128)(2,1)S(1)} %get-tuple-element.19.rest_0_.rest_2_), channel_id=1, source_target_pairs={{0,2},{2,0},{1,3},{3,1},{4,6},{6,4},{5,7},{7,5},{8,10},{10,8},{9,1... | collective-permute-start | bytes 3145736 | tf_op jit(solution)/shard_map/ppermute | solution.py:359
  6.5 35.2 %collective-permute-start.7 = (bf16[2,64,2048]{2,1,0:T(8,128)(2,1)}, bf16[2,64,2048]{2,1,0:T(8,128)(2,1)}, u32[]{:S(2)}, u32[]{:S(2)}) collective-permute-start(bf16[2,64,2048]{2,1,0:T(8,128)(2,1)} %get-tuple-element.21.rest_0_), channel_id=1, source_target_pairs={{4,8},{8,4},{5,9},{9,5},{6,10},{10,6},{7,11},{11,7},{20,24},{24,20... | collective-permute-start | bytes 1572872 | tf_op jit(solution)/shard_map/ppermute | solution.py:383
  19.3 22.5 %collective-permute-start = (bf16[2,2,128,512]{3,2,1,0:T(8,128)(2,1)}, bf16[2,2,128,512]{3,2,1,0:T(8,128)(2,1)}, u32[]{:S(2)}, u32[]{:S(2)}) collective-permute-start(bf16[2,2,128,512]{3,2,1,0:T(8,128)(2,1)} %shard_map.96), channel_id=1, source_target_pairs={{0,4},{4,0},{8,12},{12,8},{1,5},{5,1},{9,13},{13,9},{2,6},{6,2},{1... | collective-permute-start | bytes 1572872 | tf_op jit(solution)/shard_map/ppermute | solution.py:399
  19.3 99.5 %collective-permute-start.19 = (bf16[2,64,2048]{2,1,0:T(8,128)(2,1)}, bf16[2,64,2048]{2,1,0:T(8,128)(2,1)}, u32[]{:S(2)}, u32[]{:S(2)}) collective-permute-start(bf16[2,64,2048]{2,1,0:T(8,128)(2,1)} %get-tuple-element.20.rest_0_), channel_id=1, source_target_pairs={{4,8},{8,4},{5,9},{9,5},{6,10},{10,6},{7,11},{11,7},{20,24},{24,20... | collective-permute-start | bytes 1572872 | tf_op jit(solution)/shard_map/ppermute | solution.py:383
  35.9 24.2 %collective-permute-start.2 = (bf16[2,2,128,512]{3,2,1,0:T(8,128)(2,1)S(1)}, bf16[2,2,128,512]{3,2,1,0:T(8,128)(2,1)S(1)}, u32[]{:S(2)}, u32[]{:S(2)}) collective-permute-start(bf16[2,2,128,512]{3,2,1,0:T(8,128)(2,1)S(1)} %shard_map.98), channel_id=1, source_target_pairs={{0,4},{4,0},{8,12},{12,8},{1,5},{5,1},{9,13},{13,9},{2,6},{6,2},{1... | collective-permute-start | bytes 1572872 | tf_op jit(solution)/shard_map/ppermute | solution.py:399
  41.7 74.5 %collective-permute-start.18 = (bf16[2,64,2048]{2,1,0:T(8,128)(2,1)}, bf16[2,64,2048]{2,1,0:T(8,128)(2,1)S(1)}, u32[]{:S(2)}, u32[]{:S(2)}) collective-permute-start(bf16[2,64,2048]{2,1,0:T(8,128)(2,1)} %get-tuple-element.20.rest_0_), channel_id=1, source_target_pairs={{0,4},{4,0},{8,12},{12,8},{1,5},{5,1},{9,13},{13,9},{2,6},{6,2},{1... | collective-permute-start | bytes 1572872 | tf_op jit(solution)/shard_map/ppermute | solution.py:382
  41.7 46.4 %collective-permute-start.8 = (bf16[2,64,2048]{2,1,0:T(8,128)(2,1)}, bf16[2,64,2048]{2,1,0:T(8,128)(2,1)S(1)}, u32[]{:S(2)}, u32[]{:S(2)}) collective-permute-start(bf16[2,64,2048]{2,1,0:T(8,128)(2,1)} %collective-permute-done.7.rest_2_), channel_id=1, source_target_pairs={{4,0},{8,12},{5,1},{9,13},{6,2},{10,14},{7,3},{11,15},{20,16},{24,... | collective-permute-start | bytes 1572872 | tf_op jit(solution)/shard_map/ppermute | solution.py:385
  44.1 52.7 %collective-permute-start.10 = (bf16[2,64,2048]{2,1,0:T(8,128)(2,1)S(1)}, bf16[2,64,2048]{2,1,0:T(8,128)(2,1)S(1)}, u32[]{:S(2)}, u32[]{:S(2)}) collective-permute-start(bf16[2,64,2048]{2,1,0:T(8,128)(2,1)S(1)} %collective-permute-done.9.rest_4_), channel_id=1, source_target_pairs={{4,0},{8,12},{5,1},{9,13},{6,2},{10,14},{7,3},{11,15},{20,16},{24,... | collective-permute-start | bytes 1572872 | tf_op jit(solution)/shard_map/ppermute | solution.py:386
  60.2 56.7 %collective-permute-start.3 = (bf16[2,2,128,512]{3,2,1,0:T(8,128)(2,1)S(1)}, bf16[2,2,128,512]{3,2,1,0:T(8,128)(2,1)S(1)}, u32[]{:S(2)}, u32[]{:S(2)}) collective-permute-start(bf16[2,2,128,512]{3,2,1,0:T(8,128)(2,1)S(1)} %pad_maximum_fusion), channel_id=1, source_target_pairs={{0,8},{4,12},{8,0},{12,4},{1,9},{5,13},{9,1},{13,5},{2,10},{6,14},... | collective-permute-start | bytes 1572872 | tf_op jit(solution)/shard_map/ppermute | solution.py:399
  105.4 26.1 %collective-permute-start.11 = (bf16[2,1024,256]{2,1,0:T(8,128)(2,1)S(1)}, bf16[2,1024,256]{2,1,0:T(8,128)(2,1)S(1)}, u32[]{:S(2)}, u32[]{:S(2)}) collective-permute-start(bf16[2,1024,256]{2,1,0:T(8,128)(2,1)S(1)} %shard_map.99.rest_0_), channel_id=1, source_target_pairs={{0,2},{2,0},{1,3},{3,1},{4,6},{6,4},{5,7},{7,5},{8,10},{10,8},{9,1... | collective-permute-start | bytes 3145736 | tf_op jit(solution)/shard_map/ppermute | solution.py:359
  114.7 39.3 %collective-permute-start.12 = (bf16[2,1024,256]{2,1,0:T(8,128)(2,1)S(1)}, bf16[2,1024,256]{2,1,0:T(8,128)(2,1)S(1)}, u32[]{:S(2)}, u32[]{:S(2)}) collective-permute-start(bf16[2,1024,256]{2,1,0:T(8,128)(2,1)S(1)} %shard_map.100.rest_1_), channel_id=1, source_target_pairs={{0,2},{2,0},{1,3},{3,1},{4,6},{6,4},{5,7},{7,5},{8,10},{10,8},{9,1... | collective-permute-start | bytes 3145736 | tf_op jit(solution)/shard_map/ppermute | solution.py:359
  116.2 56.8 %collective-permute-start.14 = (bf16[2,128,2048]{2,1,0:T(8,128)(2,1)S(1)}, bf16[2,128,2048]{2,1,0:T(8,128)(2,1)S(1)}, u32[]{:S(2)}, u32[]{:S(2)}) collective-permute-start(bf16[2,128,2048]{2,1,0:T(8,128)(2,1)S(1)} %get-tuple-element.18.rest_2_.rest_3_), channel_id=1, source_target_pairs={{0,2},{2,0},{1,3},{3,1},{4,6},{6,4},{5,7},{7,5},{8,10},{10,8},{9,1... | collective-permute-start | bytes 3145736 | tf_op jit(solution)/shard_map/ppermute | solution.py:359
  118.8 35.2 %collective-permute-start.4 = (bf16[2,2,128,512]{3,2,1,0:T(8,128)(2,1)S(1)}, bf16[2,2,128,512]{3,2,1,0:T(8,128)(2,1)S(1)}, u32[]{:S(2)}, u32[]{:S(2)}) collective-permute-start(bf16[2,2,128,512]{3,2,1,0:T(8,128)(2,1)S(1)} %pad_maximum_fusion.1.y), channel_id=1, source_target_pairs={{0,8},{4,12},{8,0},{12,4},{1,9},{5,13},{9,1},{13,5},{2,10},{6,14},... | collective-permute-start | bytes 1572872 | tf_op jit(solution)/shard_map/ppermute | solution.py:399
  123.8 85.7 %collective-permute-start.20 = (bf16[2,64,2048]{2,1,0:T(8,128)(2,1)}, bf16[2,64,2048]{2,1,0:T(8,128)(2,1)S(1)}, u32[]{:S(2)}, u32[]{:S(2)}) collective-permute-start(bf16[2,64,2048]{2,1,0:T(8,128)(2,1)} %collective-permute-done.19.rest_2_), channel_id=1, source_target_pairs={{4,0},{8,12},{5,1},{9,13},{6,2},{10,14},{7,3},{11,15},{20,16},{24,... | collective-permute-start | bytes 1572872 | tf_op jit(solution)/shard_map/ppermute | solution.py:385
  131.5 78.0 %collective-permute-start.22 = (bf16[2,64,2048]{2,1,0:T(8,128)(2,1)S(1)}, bf16[2,64,2048]{2,1,0:T(8,128)(2,1)S(1)}, u32[]{:S(2)}, u32[]{:S(2)}) collective-permute-start(bf16[2,64,2048]{2,1,0:T(8,128)(2,1)S(1)} %collective-permute-done.21.rest_4_), channel_id=1, source_target_pairs={{4,0},{8,12},{5,1},{9,13},{6,2},{10,14},{7,3},{11,15},{20,16},{24,... | collective-permute-start | bytes 1572872 | tf_op jit(solution)/shard_map/ppermute | solution.py:386
  154.0 30.5 %collective-permute-start.13 = (bf16[2,2,128,512]{3,2,1,0:T(8,128)(2,1)S(1)}, bf16[2,2,128,512]{3,2,1,0:T(8,128)(2,1)S(1)}, u32[]{:S(2)}, u32[]{:S(2)}) collective-permute-start(bf16[2,2,128,512]{3,2,1,0:T(8,128)(2,1)S(1)} %pad_maximum_fusion.1.y), channel_id=1, source_target_pairs={{0,4},{4,0},{8,12},{12,8},{1,5},{5,1},{9,13},{13,9},{2,6},{6,2},{1... | collective-permute-start | bytes 1572872 | tf_op jit(solution)/shard_map/ppermute | solution.py:399
  154.0 46.9 %collective-permute-start.5 = (bf16[2,2,128,512]{3,2,1,0:T(8,128)(2,1)S(1)}, bf16[2,2,128,512]{3,2,1,0:T(8,128)(2,1)S(1)}, u32[]{:S(2)}, u32[]{:S(2)}) collective-permute-start(bf16[2,2,128,512]{3,2,1,0:T(8,128)(2,1)S(1)} %collective-permute-done.4.y), channel_id=1, source_target_pairs={{0,4},{4,0},{8,12},{12,8},{1,5},{5,1},{9,13},{13,9},{2,6},{6,2},{1... | collective-permute-start | bytes 1572872 | tf_op jit(solution)/shard_map/ppermute | solution.py:399
  241.9 27.3 %collective-permute-start.15 = (bf16[2,256,512]{2,1,0:T(8,128)(2,1)}, bf16[2,256,512]{2,1,0:T(8,128)(2,1)S(1)}, u32[]{:S(2)}, u32[]{:S(2)}) collective-permute-start(bf16[2,256,512]{2,1,0:T(8,128)(2,1)} %copy-done.5), channel_id=1, source_target_pairs={{0,4},{4,0},{8,12},{12,8},{1,5},{5,1},{9,13},{13,9},{2,6},{6,2},{1... | collective-permute-start | bytes 1572872 | tf_op jit(solution)/shard_map/ppermute | solution.py:399
  242.7 26.1 %collective-permute-start.24 = (bf16[2,512,256]{2,1,0:T(8,128)(2,1)S(1)}, bf16[2,512,256]{2,1,0:T(8,128)(2,1)S(1)}, u32[]{:S(2)}, u32[]{:S(2)}) collective-permute-start(bf16[2,512,256]{2,1,0:T(8,128)(2,1)S(1)} %shard_map.106.rest_1_), channel_id=1, source_target_pairs={{0,2},{2,0},{1,3},{3,1},{4,6},{6,4},{5,7},{7,5},{8,10},{10,8},{9,1... | collective-permute-start | bytes 1572872 | tf_op jit(solution)/shard_map/ppermute | solution.py:359
  244.2 24.6 %collective-permute-start.25 = (bf16[2,512,256]{2,1,0:T(8,128)(2,1)S(1)}, bf16[2,512,256]{2,1,0:T(8,128)(2,1)S(1)}, u32[]{:S(2)}, u32[]{:S(2)}) collective-permute-start(bf16[2,512,256]{2,1,0:T(8,128)(2,1)S(1)} %shard_map.107.rest_2_), channel_id=1, source_target_pairs={{0,2},{2,0},{1,3},{3,1},{4,6},{6,4},{5,7},{7,5},{8,10},{10,8},{9,1... | collective-permute-start | bytes 1572872 | tf_op jit(solution)/shard_map/ppermute | solution.py:359
  254.5 40.2 %collective-permute-start.23 = (bf16[2,1024,256]{2,1,0:T(8,128)(2,1)S(1)}, bf16[2,1024,256]{2,1,0:T(8,128)(2,1)S(1)}, u32[]{:S(2)}, u32[]{:S(2)}) collective-permute-start(bf16[2,1024,256]{2,1,0:T(8,128)(2,1)S(1)} %shard_map.105.rest_0_), channel_id=1, source_target_pairs={{0,2},{2,0},{1,3},{3,1},{4,6},{6,4},{5,7},{7,5},{8,10},{10,8},{9,1... | collective-permute-start | bytes 3145736 | tf_op jit(solution)/shard_map/ppermute | solution.py:359
  265.4 26.1 %collective-permute-start.17 = (bf16[2,256,512]{2,1,0:T(8,128)(2,1)S(1)}, bf16[2,256,512]{2,1,0:T(8,128)(2,1)S(1)}, u32[]{:S(2)}, u32[]{:S(2)}) collective-permute-start(bf16[2,256,512]{2,1,0:T(8,128)(2,1)S(1)} %add_convert_fusion.6), channel_id=1, source_target_pairs={{0,8},{4,12},{8,0},{12,4},{1,9},{5,13},{9,1},{13,5},{2,10},{6,14},... | collective-permute-start | bytes 1572872 | tf_op jit(solution)/shard_map/ppermute | solution.py:399
  291.7 23.7 %collective-permute-start.27 = (bf16[2,256,512]{2,1,0:T(8,128)(2,1)S(1)}, bf16[2,256,512]{2,1,0:T(8,128)(2,1)S(1)}, u32[]{:S(2)}, u32[]{:S(2)}) collective-permute-start(bf16[2,256,512]{2,1,0:T(8,128)(2,1)S(1)} %add_convert_fusion.5.y), channel_id=1, source_target_pairs={{0,8},{4,12},{8,0},{12,4},{1,9},{5,13},{9,1},{13,5},{2,10},{6,14},... | collective-permute-start | bytes 1572872 | tf_op jit(solution)/shard_map/ppermute | solution.py:399
  291.9 29.7 %collective-permute-start.26 = (bf16[2,256,512]{2,1,0:T(8,128)(2,1)S(1)}, bf16[2,256,512]{2,1,0:T(8,128)(2,1)S(1)}, u32[]{:S(2)}, u32[]{:S(2)}) collective-permute-start(bf16[2,256,512]{2,1,0:T(8,128)(2,1)S(1)} %add_convert_fusion.5.y), channel_id=1, source_target_pairs={{0,4},{4,0},{8,12},{12,8},{1,5},{5,1},{9,13},{13,9},{2,6},{6,2},{1... | collective-permute-start | bytes 1572872 | tf_op jit(solution)/shard_map/ppermute | solution.py:399
  (23 other events, 277.8 us)
